TPU v7x, 256 devices: a whole 4x4x8 slice. The times are simulated.
256 devices in a mesh: gr: 16 (over x, y_hi, core), gc: 16 (over y_lo, z).
Axes of the slice: x: 4, y: 4 (y_hi: 2, y_lo: 2; y = y_hi * 2 + y_lo), z: 8, core: 2. Of those that a mesh axis runs over, the one named last changes fastest.
Arguments:
- border: bfloat16 [96, 768, 2048], P('gc', None, 'gr'), may hold values from -1 to 1
- row_scale: float32 [96, 768], P('gc'), may hold values from 0.1 to 10
- block_pick: int32 [96, 16], replicated, may hold values from 0 to 3
- given_diag: float32 [8192], replicated, may hold values from 0.5 to 4
Outputs:
- factored: float32 [8192, 8192], P('gr', 'gc')
All inputs are finite; a program needn't handle non-finite values.
Results may differ from a plain program's by a relative error of at most 0.00097.
Values may be sent and summed in bfloat16 or wider, within the bound.
No kernel may reach another device: no remote copies, remote signals or barrier semaphores. Data moves between devices by JAX's collectives and lax.ppermute only.
A program may use at most 128 MiB of HBM per device.

v0:
```python
import jax
import jax.numpy as jnp
from jax import lax
from jax.sharding import PartitionSpec as P

N = 8192
BLK = 128
NWIN = 16
PW = 256
PANELS = 2


def broadcast(x, axis, root):
    mine = lax.axis_index(axis) == root
    return lax.psum(jnp.where(mine, x, jnp.zeros_like(x)), axis)


def place_tiles(row_pick, col_pick, gram_tiles, span_count):
    positions = jnp.arange(span_count, dtype=jnp.int32)
    rows_hot = (row_pick[:, :, None] == positions[None, None, :]).astype(jnp.float32)
    cols_hot = (col_pick[:, :, None] == positions[None, None, :]).astype(jnp.float32)
    pair_hot = jnp.einsum("sam,sbn->sambn", rows_hot, cols_hot)
    return jnp.einsum("sambn,saxby->amxbny", pair_hot, gram_tiles, precision=lax.Precision.HIGHEST)


def body(border, row_scale, block_pick, given_diag):
    grid_rows = lax.axis_size("gr")
    grid_cols = lax.axis_size("gc")
    row_index = lax.axis_index("gr")
    col_index = lax.axis_index("gc")
    scen_here = border.shape[0]
    row_windows = NWIN // grid_rows
    col_windows = NWIN // grid_cols
    span_count = N // (BLK * NWIN)
    local_rows = N // grid_rows
    local_cols = N // grid_cols
    scaled = (jnp.sqrt(row_scale)[:, :, None] * border).astype(jnp.bfloat16)
    gram_rows = jnp.einsum(
        "srx,sry->sxy",
        scaled,
        lax.all_gather(scaled, "gr", axis=2, tiled=True),
        preferred_element_type=jnp.float32,
    )
    gram_tiles = gram_rows.reshape(scen_here, row_windows, BLK, NWIN, BLK)
    received = lax.all_to_all(gram_tiles, "gc", split_axis=3, concat_axis=0, tiled=True)
    row_pick = lax.dynamic_slice_in_dim(block_pick, row_index * row_windows, row_windows, 1)
    col_pick = lax.dynamic_slice_in_dim(block_pick, col_index * col_windows, col_windows, 1)
    placed = place_tiles(row_pick, col_pick, received, span_count)
    assembled = placed.reshape(local_rows, local_cols)
    row_global = row_index * local_rows + jnp.arange(local_rows, dtype=jnp.int32)
    col_global = col_index * local_cols + jnp.arange(local_cols, dtype=jnp.int32)
    diag_here = lax.dynamic_slice_in_dim(given_diag, row_index * local_rows, local_rows, 0)
    factored = assembled + jnp.where(
        row_global[:, None] == col_global[None, :], diag_here[:, None], 0.0
    )
    row_ratio = grid_rows // grid_cols
    for panel_index in range(PANELS):
        first_col = panel_index * PW
        past_col = first_col + PW
        corner = broadcast(factored[first_col:past_col, first_col:past_col], "gr", 0)
        chol_block = jnp.linalg.cholesky(corner)
        solved = jax.scipy.linalg.solve_triangular(
            chol_block, factored[:, first_col:past_col].T, lower=True
        ).T
        padded = jnp.zeros((local_rows, PW), jnp.float32).at[first_col:past_col].set(chol_block)
        row_inside = (row_global >= first_col) & (row_global < past_col)
        solved = jnp.where(
            (row_global >= past_col)[:, None], solved, jnp.where(row_inside[:, None], padded, 0.0)
        )
        panel_rows = broadcast(solved, "gc", 0)
        col_inside = (col_global >= first_col) & (col_global < past_col)
        pieces = broadcast(panel_rows, "gr", col_index * row_ratio + 0)
        product = jnp.dot(
            panel_rows,
            pieces.T,
            precision=lax.Precision.HIGHEST,
            preferred_element_type=jnp.float32,
        )
        trailing = (row_global >= past_col)[:, None] & (col_global >= past_col)[None, :]
        placed_cols = (
            jnp.zeros((local_rows, local_cols), jnp.float32)
            .at[:, first_col:past_col]
            .set(panel_rows)
        )
        factored = jnp.where(trailing, factored - product, factored)
        factored = jnp.where(col_inside[None, :], placed_cols, factored)
        factored = jnp.where(row_inside[:, None] & (col_global >= past_col)[None, :], 0.0, factored)
    return factored


def solution(mesh):
    in_specs = (P("gc", None, "gr"), P("gc", None), P(), P())
    out_specs = P("gr", "gc")
    return jax.shard_map(body, mesh=mesh, in_specs=in_specs, out_specs=out_specs, check_vma=False)
```

profile of v0, /device:TPU:1, one launch (start us, length us, event | category | flops | bytes accessed | tf_op | source)
XLA Modules:
  0.0 1326.2 jit_solution(5797193775737873356)
XLA Ops:
  7.3 2.7 multiply_convert_fusion
  10.0 142.5 %all-gather.2.cloned.1.call-done = bf16[6,768,2048]{2,1,0:T(8,128)(2,1)} async-done(((bf16[6,768,128]{2,1,0:T(8,128)(2,1)}), bf16[6,768,2048]{2,1,0:T(8,128)(2,1)}) %all-gather.2.cloned.1.call-update) | async-done | bytes 18874384 | tf_op jit(solution)/shard_map/all_gather | solution.py:41
  152.5 8.3 fusion.63
  160.8 1.5 copy.63
  162.2 4.6 copy.39
  166.8 6.9 all-to-all-start
  175.4 138.1 %all-to-all-done = f32[6,1,128,16,128]{4,2,0,1,3:T(8,128)} async-done(((f32[6,1,128,16,128]{4,2,0,1,3:T(8,128)}), f32[6,1,128,16,128]{4,2,0,1,3:T(8,128)}, u32[]{:S(2)}, u32[]{:S(2)}) %all-to-all-start) | async-done | bytes 6291488 | tf_op jit(solution)/shard_map/all_to_all | solution.py:45
  313.5 9.6 fusion.2
  324.8 145.2 %all-reduce.12.cloned.1.call-done = f32[256,256]{0,1:T(8,128)} async-done(((f32[256,256]{0,1:T(8,128)}), f32[256,256]{0,1:T(8,128)}) %all-reduce.12.cloned.1.call-update) | async-done | bytes 262160 | tf_op jit(solution)/shard_map/psum | solution.py:15
  472.1 11.7 cholesky.130
  484.0 9.8 custom-call.13
  494.4 11.7 cholesky.147
  509.1 4.6 while.8
  510.0 1.4 dynamic-slice.50
  512.1 1.4 dynamic-slice.50
  513.7 19.7 %custom-call.14 = f32[2,128,128]{1,2,0:T(8,128)S(1)} custom-call(f32[2,128,128]{2,1,0:T(8,128)S(1)} %get-tuple-element.69), custom_call_target="InvertDiagBlocksLowerTriangular" | custom-call | tf_op jit(solution)/shard_map/jit(_solve_triangular)/triangular_solve | solution.py:62
  536.3 126.2 %all-reduce.14.cloned.1.call-done = f32[512,256]{0,1:T(8,128)} async-done(((f32[512,256]{0,1:T(8,128)}), f32[512,256]{0,1:T(8,128)}) %all-reduce.14.cloned.1.call-update) | async-done | bytes 524304 | tf_op jit(solution)/shard_map/psum | solution.py:15
  662.5 2.7 broadcast_select_fusion.2
  665.2 153.1 %all-reduce.16.cloned.1.call-done = f32[512,256]{0,1:T(8,128)} async-done(((f32[512,256]{0,1:T(8,128)}), f32[512,256]{0,1:T(8,128)}) %all-reduce.16.cloned.1.call-update) | async-done | bytes 524304 | tf_op jit(solution)/shard_map/psum | solution.py:15
  818.3 2.5 fusion.8
  821.7 145.3 %all-reduce.18.cloned.1.call-done = f32[256,256]{0,1:T(8,128)} async-done(((f32[256,256]{0,1:T(8,128)}), f32[256,256]{0,1:T(8,128)}) %all-reduce.18.cloned.1.call-update) | async-done | bytes 262160 | tf_op jit(solution)/shard_map/psum | solution.py:15
  969.0 11.7 cholesky.164
  980.9 9.8 custom-call.15
  991.3 11.7 cholesky.181
  1005.9 4.6 while.9
  1006.8 1.4 dynamic-slice.52
  1009.0 1.4 dynamic-slice.52
  1010.5 19.7 %custom-call.16 = f32[2,128,128]{1,2,0:T(8,128)S(1)} custom-call(f32[2,128,128]{2,1,0:T(8,128)S(1)} %get-tuple-element.70), custom_call_target="InvertDiagBlocksLowerTriangular" | custom-call | tf_op jit(solution)/shard_map/jit(_solve_triangular)/triangular_solve | solution.py:62
  1032.5 126.9 %all-reduce.20.cloned.1.call-done = f32[512,256]{0,1:T(8,128)} async-done(((f32[512,256]{0,1:T(8,128)}), f32[512,256]{0,1:T(8,128)}) %all-reduce.20.cloned.1.call-update) | async-done | bytes 524304 | tf_op jit(solution)/shard_map/psum | solution.py:15
  1160.2 154.7 %all-reduce.22.cloned.1.call-done = f32[512,256]{0,1:T(8,128)} async-done(((f32[512,256]{0,1:T(8,128)}), f32[512,256]{0,1:T(8,128)}) %all-reduce.22.cloned.1.call-update) | async-done | bytes 524304 | tf_op jit(solution)/shard_map/psum | solution.py:15
  1315.0 2.7 fusion.6
  1317.6 1.3 copy.54
  (95 shorter events, 22.5 us)
Async XLA Ops:
  6.5 146.0 %all-gather.2.cloned.1.call-start = ((), (), s32[]{:S(2)}) async-start(), calls=%async_computation.1 | async-start | bytes 20054016 | tf_op jit(solution)/shard_map/all_gather | solution.py:41
  166.8 146.7 %all-to-all-start = ((f32[6,1,128,16,128]{4,2,0,1,3:T(8,128)}), f32[6,1,128,16,128]{4,2,0,1,3:T(8,128)}, u32[]{:S(2)}, u32[]{:S(2)}) async-start(f32[6,1,128,16,128]{4,2,0,1,3:T(8,128)} %copy.39), calls=%async_computation | async-start | bytes 12582912 | tf_op jit(solution)/shard_map/all_to_all | solution.py:45
  173.7 296.3 %all-reduce.12.cloned.1.call-start = ((), (), s32[]{:S(2)}) async-start(), calls=%async_computation.2 | async-start | bytes 524288 | tf_op jit(solution)/shard_map/psum | solution.py:15
  324.6 337.9 %all-reduce.14.cloned.1.call-start = ((), (), s32[]{:S(2)}) async-start(), calls=%async_computation.3 | async-start | bytes 1048576 | tf_op jit(solution)/shard_map/psum | solution.py:15
  535.5 282.8 %all-reduce.16.cloned.1.call-start = ((), (), s32[]{:S(2)}) async-start(), calls=%async_computation.4 | async-start | bytes 1048576 | tf_op jit(solution)/shard_map/psum | solution.py:15
  665.2 301.8 %all-reduce.18.cloned.1.call-start = ((), (), s32[]{:S(2)}) async-start(), calls=%async_computation.5 | async-start | bytes 524288 | tf_op jit(solution)/shard_map/psum | solution.py:15
  821.6 337.8 %all-reduce.20.cloned.1.call-start = ((), (), s32[]{:S(2)}) async-start(), calls=%async_computation.6 | async-start | bytes 1048576 | tf_op jit(solution)/shard_map/psum | solution.py:15
  1032.4 282.6 %all-reduce.22.cloned.1.call-start = ((), (), s32[]{:S(2)}) async-start(), calls=%async_computation.7 | async-start | bytes 1048576 | tf_op jit(solution)/shard_map/psum | solution.py:15
Sparse Core Ops, SparseCore 0:
  10.1 142.3 all-gather.1
  324.7 145.3 all-reduce.11
  535.7 126.7 all-reduce.13
  665.3 152.9 all-reduce.15
  821.7 145.2 all-reduce.17
  1032.5 126.7 all-reduce.19
  1162.0 152.9 all-reduce.21
where the time goes:
time: 1330 us
  waiting for transfers between devices  1130 us (85%)
  other arithmetic  121 us (9%)
  matrix products  26.5 us (2%)
  local copies, waits for them, and re-layouts  21.6 us (2%)
  between operations  17 us (1%)
    psum x6, waiting for transfers between devices, broadcast(): return lax.psum(jnp.where(mine, x, jnp.zeros_like(x)), axis)  851 us
    all_gather x1, waiting for transfers between devices, body(): lax.all_gather(scaled, 'gr', axis=2, tiled=True)  143 us
    all_to_all x1, waiting for transfers between devices, body(): lax.all_to_all(gram_tiles, 'gc', split_axis=3, concat_axis=0, tiled=True)  138 us
    another operation x14, other arithmetic, body(): chol_block = jnp.linalg.cholesky(corner)  69.3 us
    another operation x3, other arithmetic, body(): jax.scipy.linalg.solve_triangular(chol_block, factored[:, first_col:past_...  39.4 us
  transfers between devices with their start and end apart: 8, of which 8 were waited for; matrix products, arithmetic and copies ran while one was open for 0% of the time, Pallas kernels for 0%

commit v1 on v0

--- a/solution.py
+++ b/solution.py
@@ -12,7 +12,7 @@
 
 def broadcast(x, axis, root):
     mine = lax.axis_index(axis) == root
-    return lax.psum(jnp.where(mine, x, jnp.zeros_like(x)), axis)
+    return jax.lax.all_gather(jnp.where(mine, x, jnp.zeros_like(x)), axis).sum(axis=0)
 
 
 def place_tiles(row_pick, col_pick, gram_tiles, span_count):

time: 1330 us -> 969 us (0.73)
  waiting for transfers between devices: 1130 us -> 753 us
  other arithmetic: 121 us -> 139 us
    psum x6 -> x0, waiting for transfers between devices: 851 us -> none  [broadcast(): return lax.psum(jnp.where(mine, x, jnp.zeros_like(x)), axis)]
    all_gather x0 -> x6, waiting for transfers between devices: none -> 472 us  [broadcast(): jax.lax.all_gather(jnp.where(mine, x, jnp.zeros_like(x)), axis).sum(axis=0)]
    reduce_sum x0 -> x6, other arithmetic: none -> 20.9 us  [broadcast(): jax.lax.all_gather(jnp.where(mine, x, jnp.zeros_like(x)), axis).sum(axis=0)]
where the time goes in v1:
time: 969 us; the launch traced here: 961 us
  waiting for transfers between devices  753 us (78%)
  other arithmetic  139 us (14%)
  matrix products  26.2 us (3%)
  local copies, waits for them, and re-layouts  17.3 us (2%)
  between operations  17.1 us (2%)
    all_gather x6, waiting for transfers between devices, broadcast(): jax.lax.all_gather(jnp.where(mine, x, jnp.zeros_like(x)), axis).sum(axis=0)  472 us
    all_gather x1, waiting for transfers between devices, body(): lax.all_gather(scaled, 'gr', axis=2, tiled=True)  143 us
    all_to_all x1, waiting for transfers between devices, body(): lax.all_to_all(gram_tiles, 'gc', split_axis=3, concat_axis=0, tiled=True)  138 us
    another operation x14, other arithmetic, body(): chol_block = jnp.linalg.cholesky(corner)  69.3 us
    another operation x3, other arithmetic, body(): jax.scipy.linalg.solve_triangular(chol_block, factored[:, first_col:past_...  39.4 us
    reduce_sum x6, other arithmetic, broadcast(): jax.lax.all_gather(jnp.where(mine, x, jnp.zeros_like(x)), axis).sum(axis=0)  20.9 us
  transfers between devices with their start and end apart: 8, of which 8 were waited for; matrix products, arithmetic and copies ran while one was open for 0% of the time, Pallas kernels for 0%

profile of v1, /device:TPU:1, one launch (start us, length us, event | category | flops | bytes accessed | tf_op | source)
XLA Modules:
  0.0 961.2 jit_solution(10918788772692299019)
XLA Ops:
  7.3 2.7 multiply_convert_fusion
  10.0 142.5 %all-gather.14.cloned.1.call-done = bf16[6,768,2048]{2,1,0:T(8,128)(2,1)} async-done(((bf16[6,768,128]{2,1,0:T(8,128)(2,1)}), bf16[6,768,2048]{2,1,0:T(8,128)(2,1)}) %all-gather.14.cloned.1.call-update) | async-done | bytes 18874384 | tf_op jit(solution)/shard_map/all_gather | solution.py:41
  152.5 8.3 fusion.63
  162.2 4.6 copy.25
  166.8 6.9 all-to-all-start
  175.3 138.1 %all-to-all-done = f32[6,1,128,16,128]{4,2,0,1,3:T(8,128)} async-done(((f32[6,1,128,16,128]{4,2,0,1,3:T(8,128)}), f32[6,1,128,16,128]{4,2,0,1,3:T(8,128)}, u32[]{:S(2)}, u32[]{:S(2)}) %all-to-all-start) | async-done | bytes 6291488 | tf_op jit(solution)/shard_map/all_to_all | solution.py:45
  313.5 9.6 %fusion.2 = f32[1,4,128,1,4,128]{5,4,1,2,3,0:T(4,128)S(1)} fusion(f32[96,128,128,1]{2,1,0,3:T(8,128)} %bitcast.3, f32[96,4]{0,1:T(4,128)S(1)} %get-tuple-element.114, f32[96,4]{0,1:T(4,128)S(1)} %get-tuple-element.113), kind=kOutput, calls=%fused_computation.9 | convolution fusion | flops 301991424 | bytes 7343104 | tf_op jit(solution)/shard_map/sambn,saxby->amxbny/dot_general | solution.py:23
  324.6 63.0 %all-gather.16.cloned.1.call-done = f32[4096,256]{1,0:T(8,128)} async-done(((f32[256,256]{1,0:T(8,128)}), f32[4096,256]{1,0:T(8,128)}) %all-gather.16.cloned.1.call-update) | async-done | bytes 4194320 | tf_op jit(solution)/shard_map/all_gather | solution.py:15
  387.6 2.5 reduce_sum.54
  390.3 11.7 %cholesky.130 = f32[128,128]{1,0:T(8,128)S(1)} custom-call(f32[128,128]{1,0:T(8,128)S(1)} %cholesky.194), custom_call_target="Cholesky" | custom-call | tf_op jit(solution)/shard_map/jit(cholesky)/cholesky | solution.py:61
  402.1 9.8 %custom-call.13 = f32[1,128,128]{1,2,0:T(8,128)S(1)} custom-call(f32[1,128,128]{2,1,0:T(8,128)S(1)} %get-tuple-element.106), custom_call_target="InvertDiagBlocksLowerTriangular" | custom-call | tf_op jit(solution)/shard_map/jit(cholesky)/cholesky | solution.py:61
  412.4 11.7 %cholesky.147 = f32[128,128]{1,0:T(8,128)S(1)} custom-call(f32[128,128]{1,0:T(8,128)S(1)} %convolution_subtract_fusion.3), custom_call_target="Cholesky" | custom-call | tf_op jit(solution)/shard_map/jit(cholesky)/cholesky | solution.py:61
  427.0 4.3 while.8
  431.3 19.7 %custom-call.14 = f32[2,128,128]{1,2,0:T(8,128)S(1)} custom-call(f32[2,128,128]{2,1,0:T(8,128)S(1)} %get-tuple-element.69), custom_call_target="InvertDiagBlocksLowerTriangular" | custom-call | tf_op jit(solution)/shard_map/jit(_solve_triangular)/triangular_solve | solution.py:62
  454.2 98.6 %all-gather.18.cloned.1.call-done = f32[8192,256]{1,0:T(8,128)} async-done(((f32[512,256]{1,0:T(8,128)}), f32[8192,256]{1,0:T(8,128)}) %all-gather.18.cloned.1.call-update) | async-done | bytes 8388624 | tf_op jit(solution)/shard_map/all_gather | solution.py:15
  552.9 4.0 reduce_sum.55
  556.8 1.7 broadcast_select_fusion.2
  558.7 76.2 %all-gather.20.cloned.1.call-done = f32[8192,256]{1,0:T(8,128)} async-done(((f32[512,256]{1,0:T(8,128)}), f32[8192,256]{1,0:T(8,128)}) %all-gather.20.cloned.1.call-update) | async-done | bytes 8388624 | tf_op jit(solution)/shard_map/all_gather | solution.py:15
  634.9 4.0 reduce_sum.56
  638.8 2.3 fusion.8
  642.3 58.9 %all-gather.22.cloned.1.call-done = f32[4096,256]{1,0:T(8,128)} async-done(((f32[256,256]{1,0:T(8,128)}), f32[4096,256]{1,0:T(8,128)}) %all-gather.22.cloned.1.call-update) | async-done | bytes 4194320 | tf_op jit(solution)/shard_map/all_gather | solution.py:15
  701.2 2.5 reduce_sum.57
  703.9 11.7 %cholesky.164 = f32[128,128]{1,0:T(8,128)S(1)} custom-call(f32[128,128]{1,0:T(8,128)S(1)} %cholesky.197), custom_call_target="Cholesky" | custom-call | tf_op jit(solution)/shard_map/jit(cholesky)/cholesky | solution.py:61
  715.7 9.8 %custom-call.15 = f32[1,128,128]{1,2,0:T(8,128)S(1)} custom-call(f32[1,128,128]{2,1,0:T(8,128)S(1)} %get-tuple-element.102), custom_call_target="InvertDiagBlocksLowerTriangular" | custom-call | tf_op jit(solution)/shard_map/jit(cholesky)/cholesky | solution.py:61
  726.0 11.7 %cholesky.181 = f32[128,128]{1,0:T(8,128)S(1)} custom-call(f32[128,128]{1,0:T(8,128)S(1)} %convolution_subtract_fusion.2), custom_call_target="Cholesky" | custom-call | tf_op jit(solution)/shard_map/jit(cholesky)/cholesky | solution.py:61
  740.5 4.4 while.9
  744.9 19.7 %custom-call.16 = f32[2,128,128]{1,2,0:T(8,128)S(1)} custom-call(f32[2,128,128]{2,1,0:T(8,128)S(1)} %get-tuple-element.70), custom_call_target="InvertDiagBlocksLowerTriangular" | custom-call | tf_op jit(solution)/shard_map/jit(_solve_triangular)/triangular_solve | solution.py:62
  767.2 99.3 %all-gather.24.cloned.1.call-done = f32[8192,256]{1,0:T(8,128)} async-done(((f32[512,256]{1,0:T(8,128)}), f32[8192,256]{1,0:T(8,128)}) %all-gather.24.cloned.1.call-update) | async-done | bytes 8388624 | tf_op jit(solution)/shard_map/all_gather | solution.py:15
  866.5 4.0 reduce_sum.58
  871.3 76.2 %all-gather.26.cloned.1.call-done = f32[8192,256]{1,0:T(8,128)} async-done(((f32[512,256]{1,0:T(8,128)}), f32[8192,256]{1,0:T(8,128)}) %all-gather.26.cloned.1.call-update) | async-done | bytes 8388624 | tf_op jit(solution)/shard_map/all_gather | solution.py:15
  947.6 4.0 reduce_sum.59
  951.6 2.3 fusion.6
  (84 shorter events, 25.5 us)
Async XLA Ops:
  6.5 146.0 %all-gather.14.cloned.1.call-start = ((), (), s32[]{:S(2)}) async-start(), calls=%async_computation.1 | async-start | bytes 20054016 | tf_op jit(solution)/shard_map/all_gather | solution.py:41
  166.8 146.7 %all-to-all-start = ((f32[6,1,128,16,128]{4,2,0,1,3:T(8,128)}), f32[6,1,128,16,128]{4,2,0,1,3:T(8,128)}, u32[]{:S(2)}, u32[]{:S(2)}) async-start(f32[6,1,128,16,128]{4,2,0,1,3:T(8,128)} %copy.25), calls=%async_computation | async-start | bytes 12582912 | tf_op jit(solution)/shard_map/all_to_all | solution.py:45
  173.7 213.9 %all-gather.16.cloned.1.call-start = ((), (), s32[]{:S(2)}) async-start(), calls=%async_computation.2 | async-start | bytes 4456448 | tf_op jit(solution)/shard_map/all_gather | solution.py:15
  324.3 228.6 %all-gather.18.cloned.1.call-start = ((), (), s32[]{:S(2)}) async-start(), calls=%async_computation.3 | async-start | bytes 8912896 | tf_op jit(solution)/shard_map/all_gather | solution.py:15
  453.5 181.4 %all-gather.20.cloned.1.call-start = ((), (), s32[]{:S(2)}) async-start(), calls=%async_computation.4 | async-start | bytes 8912896 | tf_op jit(solution)/shard_map/all_gather | solution.py:15
  558.6 142.6 %all-gather.22.cloned.1.call-start = ((), (), s32[]{:S(2)}) async-start(), calls=%async_computation.5 | async-start | bytes 4456448 | tf_op jit(solution)/shard_map/all_gather | solution.py:15
  641.9 224.5 %all-gather.24.cloned.1.call-start = ((), (), s32[]{:S(2)}) async-start(), calls=%async_computation.6 | async-start | bytes 8912896 | tf_op jit(solution)/shard_map/all_gather | solution.py:15
  767.1 180.4 %all-gather.26.cloned.1.call-start = ((), (), s32[]{:S(2)}) async-start(), calls=%async_computation.7 | async-start | bytes 8912896 | tf_op jit(solution)/shard_map/all_gather | solution.py:15
Sparse Core Ops, SparseCore 0:
  10.1 142.3 all-gather.13
  324.4 63.1 all-gather.15
  453.6 99.1 all-gather.17
  558.7 76.1 all-gather.19
  642.1 59.1 all-gather.21
  767.2 99.1 all-gather.23
  871.4 76.1 all-gather.25
